TPU v7x, 256 devices: a whole 4x4x8 slice. The times are simulated.
256 devices in a mesh: rad: 8 (over x_hi, y), azi: 32 (over x_lo, z, core).
Axes of the slice: x: 4 (x_hi: 2, x_lo: 2; x = x_hi * 2 + x_lo), y: 4, z: 8, core: 2. Of those that a mesh axis runs over, the one named last changes fastest.
Arguments:
- tokens: bfloat16 [64, 512, 8, 512], P('rad', 'azi'), may hold values from -6 to 6
- cotangent: bfloat16 [64, 512, 8, 512], P('rad', 'azi'), may hold values from -6 to 6
- ln_gain: float32 [512], replicated, may hold values from 0.5 to 1.5
- qkv_weight: bfloat16 [512, 1536], P('azi'), may hold values from -2 to 2
- out_weight: bfloat16 [512, 512], P('azi'), may hold values from -0.25 to 0.25
- shear_offset: int32 [1], replicated, may hold values from 0 to 511
- window_shift: int32 [3], replicated, may hold values from 1 to 7, as said below
Outputs:
- block_out: bfloat16 [64, 512, 8, 512], P('rad', 'azi')
- grad_tokens: bfloat16 [64, 512, 8, 512], P('rad', 'azi')
- grad_qkv: float32 [512, 1536], P('azi')
- grad_out: float32 [512, 512], P('azi')
- grad_gain: float32 [512], replicated
Inputs may be any that keep to these rules, and one draw needn't show every extreme that they name: `window_shift`: the radial entry lies in 1 to 3; the azimuthal and vertical entries lie in 1 to 7, and one of these two equals 7.
All inputs are finite; a program needn't handle non-finite values.
Results may differ from a plain program's by a relative error of at most 0.025.
Values may be sent and summed in bfloat16 or wider, within the bound.
A program may use at most 192 MiB of HBM per device.

v0:
```python
import jax
import jax.numpy as jnp
from jax import lax
from jax.sharding import PartitionSpec as P

HEADS = 16
HD = 32
WR = 4
WA = 8
WZ = 8
EPS = 1e-05


def shifted_2(block, axis, distance):
    devices = range(lax.axis_size(axis))
    route = [((i - distance) % len(devices), i) for i in devices]
    return lax.ppermute(block, axis, route)


def to_windows(tensor, parts):
    extent_r, extent_a, extent_z, channels = tensor.shape
    tensor = tensor.reshape(
        extent_r // WR, WR, extent_a // WA, WA, extent_z // WZ, WZ, parts, HEADS, HD
    )
    tensor = tensor.transpose(0, 2, 4, 6, 7, 1, 3, 5, 8)
    return tensor.reshape(-1, parts, HEADS, WR * WA * WZ, HD)


def from_windows(windows, extent_r, extent_a, extent_z):
    parts = windows.shape[1]
    windows = windows.reshape(
        extent_r // WR, extent_a // WA, extent_z // WZ, parts, HEADS, WR, WA, WZ, HD
    )
    windows = windows.transpose(0, 5, 1, 6, 2, 7, 3, 4, 8)
    return windows.reshape(extent_r, extent_a, extent_z, parts * HEADS * HD)


def azi_roll(pieces, amount):
    cols_dev = pieces[0].shape[1]
    device_hops = amount // cols_dev
    remainder = amount % cols_dev
    current = pieces
    bit_count = (lax.axis_size("azi") - 1).bit_length()
    for bit_level in range(bit_count):
        hopped = shifted_2((current[0], current[1]), "azi", -(1 << bit_level))
        chosen = device_hops >> bit_level & 1 == 1
        current = (
            jnp.where(chosen, hopped[0], current[0]),
            jnp.where(chosen, hopped[1], current[1]),
        )
    following = shifted_2((current[0], current[1]), "azi", -1)
    return tuple(
        (
            lax.dynamic_slice_in_dim(
                jnp.concatenate([mine, theirs], axis=1), remainder, cols_dev, 1
            )
            for mine, theirs in zip(current, following)
        )
    )


def vertical_roll(field, start):
    depth = field.shape[2]
    return lax.dynamic_slice_in_dim(jnp.concatenate([field, field], axis=2), start, depth, 2)


def shift_in(first, second, shift_rad, shift_azi, shift_ver, offset, total_cols):
    rim_rows = WR - 1
    rows_dev, cols_dev, depth, width = first.shape
    below = shifted_2((first[:rim_rows], second[:rim_rows]), "rad", -1)
    extended = (
        jnp.concatenate([first, below[0]], axis=0),
        jnp.concatenate([second, below[1]], axis=0),
    )
    leading = shifted_2((extended[0][:, : WA - 1], extended[1][:, : WA - 1]), "azi", -1)
    rolled = tuple(
        (
            lax.dynamic_slice_in_dim(
                jnp.concatenate([own_part, lead_part], axis=1), shift_azi, cols_dev, 1
            )
            for own_part, lead_part in zip(extended, leading)
        )
    )
    wrapped = azi_roll(below, (offset + shift_azi) % total_cols)
    last_row = lax.axis_index("rad") == lax.axis_size("rad") - 1
    results = []
    for rolled_part, wrapped_part in zip(rolled, wrapped):
        joined = jnp.concatenate(
            [rolled_part[:rows_dev], jnp.where(last_row, wrapped_part, rolled_part[rows_dev:])],
            axis=0,
        )
        joined = lax.dynamic_slice_in_dim(joined, shift_rad, rows_dev, 0)
        results.append(vertical_roll(joined, shift_ver))
    return (results[0], results[1])


def shift_out(first, second, shift_rad, shift_azi, shift_ver, offset, total_cols):
    rim_rows = WR - 1
    rows_dev, cols_dev, depth, width = first.shape
    above = shifted_2((first[rows_dev - rim_rows :], second[rows_dev - rim_rows :]), "rad", 1)
    extended = (
        jnp.concatenate([above[0], first], axis=0),
        jnp.concatenate([above[1], second], axis=0),
    )
    trailing = shifted_2(
        (extended[0][:, cols_dev - (WA - 1) :], extended[1][:, cols_dev - (WA - 1) :]), "azi", 1
    )
    rolled = tuple(
        (
            lax.dynamic_slice_in_dim(
                jnp.concatenate([trail_part, own_part], axis=1), WA - 1 - shift_azi, cols_dev, 1
            )
            for own_part, trail_part in zip(extended, trailing)
        )
    )
    amount = (total_cols - (offset + shift_azi) % total_cols) % total_cols
    wrapped = azi_roll(above, amount)
    first_row = lax.axis_index("rad") == 0
    results = []
    for rolled_part, wrapped_part in zip(rolled, wrapped):
        joined = jnp.concatenate(
            [jnp.where(first_row, wrapped_part, rolled_part[:rim_rows]), rolled_part[rim_rows:]],
            axis=0,
        )
        joined = lax.dynamic_slice_in_dim(joined, rim_rows - shift_rad, rows_dev, 0)
        results.append(vertical_roll(joined, depth - shift_ver))
    return (results[0], results[1])


def on_device(tokens, cotangent, ln_gain, qkv_weight, out_weight, shear_offset, window_shift):
    rows_dev, cols_dev, depth, width = tokens.shape
    number = rows_dev * cols_dev * depth
    n_rad = lax.axis_size("rad")
    n_azi = lax.axis_size("azi")
    total_cols = cols_dev * n_azi
    shift_rad = window_shift[0]
    shift_azi = window_shift[1]
    shift_ver = window_shift[2]
    offset = shear_offset[0]
    contract = (((0,), (0,)), ((), ()))
    scaling = HD ** (-0.5)
    shifted, grad_in = shift_in(
        tokens, cotangent, shift_rad, shift_azi, shift_ver, offset, total_cols
    )
    inputs_f = shifted.astype(jnp.float32).reshape(number, width)
    centre = jnp.mean(inputs_f, axis=1, keepdims=True)
    centred = inputs_f - centre
    variance = jnp.mean(centred * centred, axis=1, keepdims=True)
    inverse_std = lax.rsqrt(variance + EPS)
    normed = centred * inverse_std
    hidden = (normed * ln_gain).astype(jnp.bfloat16)
    qkv_full, out_full = (
        lax.all_gather(qkv_weight, "azi", axis=0, tiled=True),
        lax.all_gather(out_weight, "azi", axis=0, tiled=True),
    )
    qkv = jnp.dot(hidden, qkv_full, preferred_element_type=jnp.float32)
    qkv = qkv.astype(jnp.bfloat16)
    windows = to_windows(qkv.reshape(rows_dev, cols_dev, depth, 3 * width), 3)
    queries, keys_win, values = (windows[:, 0], windows[:, 1], windows[:, 2])
    scores = (
        jnp.einsum("nhqd,nhkd->nhqk", queries, keys_win, preferred_element_type=jnp.float32)
        * scaling
    )
    weights = jax.nn.softmax(scores, axis=-1)
    weights_low = weights.astype(jnp.bfloat16)
    mixed = jnp.einsum(
        "nhqk,nhkd->nhqd", weights_low, values, preferred_element_type=jnp.float32
    ).astype(jnp.bfloat16)
    attended = from_windows(mixed[:, None], rows_dev, cols_dev, depth).reshape(number, width)
    branch = jnp.dot(attended, out_full, preferred_element_type=jnp.float32)
    out_shifted = (inputs_f + branch).astype(jnp.bfloat16)
    grad_low = grad_in.reshape(number, width)
    d_attended = jnp.dot(grad_low, out_full.T, preferred_element_type=jnp.float32)
    d_attended = d_attended.astype(jnp.bfloat16)
    d_windows = to_windows(d_attended.reshape(rows_dev, cols_dev, depth, width), 1)[:, 0]
    d_weights = jnp.einsum("nhqd,nhkd->nhqk", d_windows, values, preferred_element_type=jnp.float32)
    d_values = jnp.einsum(
        "nhqk,nhqd->nhkd", weights_low, d_windows, preferred_element_type=jnp.float32
    )
    d_scores = (
        weights * (d_weights - jnp.sum(weights * d_weights, axis=-1, keepdims=True))
    ).astype(jnp.bfloat16)
    d_queries = (
        jnp.einsum("nhqk,nhkd->nhqd", d_scores, keys_win, preferred_element_type=jnp.float32)
        * scaling
    )
    d_keys = (
        jnp.einsum("nhqk,nhqd->nhkd", d_scores, queries, preferred_element_type=jnp.float32)
        * scaling
    )
    d_stack = jnp.stack([d_queries, d_keys, d_values], axis=1).astype(jnp.bfloat16)
    d_qkv = from_windows(d_stack, rows_dev, cols_dev, depth).reshape(number, 3 * width)
    d_hidden = jnp.dot(d_qkv, qkv_full.T, preferred_element_type=jnp.float32)
    d_normed = d_hidden * ln_gain
    d_branch = inverse_std * (
        d_normed
        - jnp.mean(d_normed, axis=1, keepdims=True)
        - normed * jnp.mean(d_normed * normed, axis=1, keepdims=True)
    )
    grad_shifted = (grad_low.astype(jnp.float32) + d_branch).astype(jnp.bfloat16)
    shape_out = (rows_dev, cols_dev, depth, width)
    block_out, grad_tokens = shift_out(
        out_shifted.reshape(shape_out),
        grad_shifted.reshape(shape_out),
        shift_rad,
        shift_azi,
        shift_ver,
        offset,
        total_cols,
    )
    term_qkv = lax.dot_general(hidden, d_qkv, contract, preferred_element_type=jnp.float32)
    term_out = lax.dot_general(attended, grad_low, contract, preferred_element_type=jnp.float32)
    whole_term = lax.psum(jnp.concatenate([term_qkv, term_out], axis=1).astype(jnp.bfloat16), "rad")
    share = lax.psum_scatter(whole_term, "azi", scatter_dimension=0, tiled=True).astype(jnp.float32)
    gain_total = lax.psum(jnp.sum(d_hidden * normed, axis=0), ("rad", "azi"))
    factor = float(number * n_rad * n_azi) ** (-0.5)
    grad_qkv = share[:, : 3 * width] * factor
    grad_out = share[:, 3 * width :] * factor
    return (block_out, grad_tokens, grad_qkv, grad_out, gain_total * factor)


def solution(mesh):
    in_specs = (
        P("rad", "azi", None, None),
        P("rad", "azi", None, None),
        P(),
        P("azi", None),
        P("azi", None),
        P(),
        P(),
    )
    out_specs = (
        P("rad", "azi", None, None),
        P("rad", "azi", None, None),
        P("azi", None),
        P("azi", None),
        P(),
    )
    return jax.shard_map(
        on_device, mesh=mesh, in_specs=in_specs, out_specs=out_specs, check_vma=False
    )
```

profile of v0, /device:TPU:32, one launch (start us, length us, event | category | flops | bytes accessed | tf_op | source)
XLA Modules:
  0.0 756.4 jit_solution(11868625129123604809)
XLA Ops:
  8.3 5.6 collective-permute-start.16
  15.7 7.7 %collective-permute-done.16 = bf16[3,16,8,512]{3,2,1,0:T(8,128)(2,1)} collective-permute-done((bf16[3,16,8,512]{3,2,1,0:T(8,128)(2,1)S(1)}, bf16[3,16,8,512]{3,2,1,0:T(8,128)(2,1)}, u32[]{:S(2)}, u32[]{:S(2)}) %collective-permute-start.16) | collective-permute-done | bytes 393248 | tf_op jit(solution)/shard_map/ppermute | solution.py:17
  24.0 1.4 fusion.61
  26.2 4.5 collective-permute-done
  30.7 1.4 broadcast_select_fusion
  32.1 8.7 %collective-permute-start.19 = (bf16[3,16,8,512]{3,2,1,0:T(8,128)(2,1)S(1)}, bf16[3,16,8,512]{3,2,1,0:T(8,128)(2,1)S(1)}, u32[]{:S(2)}, u32[]{:S(2)}) collective-permute-start(bf16[3,16,8,512]{3,2,1,0:T(8,128)(2,1)S(1)} %get-tuple-element.10), channel_id=1, source_target_pairs={{2,0},{3,1},{4,2},{5,3},{6,4},{7,5},{8,6},{9,7},{10,8},{11,9},{12,... | collective-permute-start | bytes 1179656 | tf_op jit(solution)/shard_map/ppermute | solution.py:17
  43.3 4.6 collective-permute-start.3
  49.3 9.5 %collective-permute-start.20 = (bf16[3,16,8,512]{3,2,1,0:T(8,128)(2,1)}, bf16[3,16,8,512]{3,2,1,0:T(8,128)(2,1)}, u32[]{:S(2)}, u32[]{:S(2)}) collective-permute-start(bf16[3,16,8,512]{3,2,1,0:T(8,128)(2,1)} %broadcast_select_fusion.2), channel_id=1, source_target_pairs={{4,0},{5,1},{6,2},{7,3},{8,4},{9,5},{10,6},{11,7},{12,8},{13,9},{1... | collective-permute-start | bytes 1179656 | tf_op jit(solution)/shard_map/ppermute | solution.py:17
  60.8 10.2 %collective-permute-start.4 = (bf16[3,16,8,512]{3,2,1,0:T(8,128)(2,1)S(1)}, bf16[3,16,8,512]{3,2,1,0:T(8,128)(2,1)}, u32[]{:S(2)}, u32[]{:S(2)}) collective-permute-start(bf16[3,16,8,512]{3,2,1,0:T(8,128)(2,1)S(1)} %broadcast_select_fusion.3), channel_id=1, source_target_pairs={{4,0},{5,1},{6,2},{7,3},{8,4},{9,5},{10,6},{11,7},{12,8},{13,9},{1... | collective-permute-start | bytes 1179656 | tf_op jit(solution)/shard_map/ppermute | solution.py:17
  71.0 7.3 collective-permute-done.20
  78.3 1.8 broadcast_select_fusion.4
  80.1 4.3 collective-permute-start.21
  84.4 70.5 %all_gather.7 = bf16[512,512]{1,0:T(8,128)(2,1)} all-gather(bf16[16,512]{1,0:T(8,128)(2,1)S(1)} %copy-done.14), channel_id=1, replica_groups=mesh['rad'=8,'azi'=32] {'azi'}, dimensions={0}, use_global_device_ids=true | all-gather | bytes 540672 | tf_op jit(solution)/shard_map/all_gather | solution.py:154
  163.7 1.7 collective-permute-start.22
  165.4 1.5 fusion.39
  166.9 19.8 %collective-permute-done.5 = bf16[3,16,8,512]{3,2,1,0:T(8,128)(2,1)S(1)} collective-permute-done((bf16[3,16,8,512]{3,2,1,0:T(8,128)(2,1)S(1)}, bf16[3,16,8,512]{3,2,1,0:T(8,128)(2,1)S(1)}, u32[]{:S(2)}, u32[]{:S(2)}) %collective-permute-start.5) | collective-permute-done | bytes 393248 | tf_op jit(solution)/shard_map/ppermute | solution.py:17
  186.8 10.8 %collective-permute-start.6 = (bf16[3,16,8,512]{3,2,1,0:T(8,128)(2,1)S(1)}, bf16[3,16,8,512]{3,2,1,0:T(8,128)(2,1)S(1)}, u32[]{:S(2)}, u32[]{:S(2)}) collective-permute-start(bf16[3,16,8,512]{3,2,1,0:T(8,128)(2,1)S(1)} %broadcast_select_fusion.7), channel_id=1, source_target_pairs={{16,0},{17,1},{18,2},{19,3},{20,4},{21,5},{22,6},{23,7},{24,8},{25... | collective-permute-start | bytes 1179656 | tf_op jit(solution)/shard_map/ppermute | solution.py:17
  198.3 7.7 %collective-permute-done.6 = bf16[3,16,8,512]{3,2,1,0:T(8,128)(2,1)S(1)} collective-permute-done((bf16[3,16,8,512]{3,2,1,0:T(8,128)(2,1)S(1)}, bf16[3,16,8,512]{3,2,1,0:T(8,128)(2,1)S(1)}, u32[]{:S(2)}, u32[]{:S(2)}) %collective-permute-start.6) | collective-permute-done | bytes 393248 | tf_op jit(solution)/shard_map/ppermute | solution.py:17
  208.4 1.7 convolution_convert_fusion.2
  210.1 5.9 reshape_reshape.14
  216.0 5.3 copy.26
  223.8 1.4 fusion.17
  225.2 4.8 convolution_convert_fusion
  230.1 14.6 %reshape_reshape.12 = bf16[2,4,2,8,1,8,3,16,32]{8,7,6,5,3,2,1,0,4:T(8,128)(2,1)} reshape(bf16[1024,1536]{1,0:T(8,128)(2,1)} %convolution_convert_fusion) | data formatting | bytes 6291456 | tf_op jit(solution)/shard_map/reshape;reshape | solution.py:22
  244.6 12.8 %copy.19 = bf16[2,4,2,8,1,8,3,16,32]{8,5,3,1,7,6,2,0,4:T(8,128)(2,1)} copy(bf16[2,4,2,8,1,8,3,16,32]{8,7,6,5,3,2,1,0,4:T(8,128)(2,1)} %reshape_reshape.12) | data formatting | bytes 6291456 | tf_op jit(solution)/shard_map/reshape;reshape | solution.py:22
  257.4 11.6 %fusion.11 = f32[4,16,256,256]{2,3,1,0:T(8,128)} fusion(bf16[4,3,16,256,32]{4,3,2,1,0:T(8,128)(2,1)} %bitcast.105), kind=kOutput, calls=%fused_computation.19 | convolution fusion | flops 268435456 | bytes 25165824 | tf_op jit(solution)/shard_map/nhqd,nhkd->nhqk/dot_general | solution.py:161
  269.0 19.6 %fusion.62 = (f32[4,16,256]{2,1,0:T(8,128)S(1)}, f32[4,16,256,256]{2,3,1,0:T(8,128)}) fusion(f32[4,16,256,256]{2,3,1,0:T(8,128)} %fusion.11), kind=kOutput, calls=%fused_computation.143 | output fusion | flops 16777472 | bytes 33619968 | tf_op jit(solution)/shard_map/sub | solution.py:164
  288.6 14.5 %multiply_reduce_fusion = (f32[4,16,256]{2,1,0:T(8,128)S(1)}, f32[4,16,256,256]{2,3,1,0:T(8,128)}) fusion(f32[4,16,256,256]{2,3,1,0:T(8,128)} %get-tuple-element.18, f32[4,16,256]{2,1,0:T(8,128)S(1)} %get-tuple-element.17, bf16[4,16,256,32]{3,2,1,0:T(8,128)(2,1)} %bitcast.120, bf16[4,3,16,256,32]{4,3,2,1,0:T(8,128)(2,1)} %bitcast.106), kind=kOutput, calls=%fused_computation.2 | convolution fusion | flops 281001984 | bytes 42074112 | tf_op jit(solution)/shard_map/nhqd,nhkd->nhqk/dot_general | solution.py:176
  303.1 11.7 %multiply_convert_fusion = bf16[4,16,256,256]{2,3,1,0:T(8,128)(2,1)S(1)} fusion(f32[4,16,256,256]{2,3,1,0:T(8,128)} %get-tuple-element.20, f32[4,16,256]{2,1,0:T(8,128)S(1)} %get-tuple-element.19, f32[4,16,256,256]{2,3,1,0:T(8,128)} %get-tuple-element.18, f32[4,16,256]{2,1,0:T(8,128)S(1)} %get-tuple-element.17), kind=kLoop, calls=%fused_computation.1 | loop fusion | flops 16777216 | bytes 42074112 | tf_op jit(solution)/shard_map/convert_element_type | solution.py:182
  314.8 3.3 copy-done
  318.0 3.7 multiply_convert_fusion.2
  321.7 7.1 multiply_convert_fusion.1
  328.9 9.3 %fusion.34 = bf16[4,16,256,32]{2,3,1,0:T(8,128)(2,1)} fusion(bf16[4,16,256,32]{3,2,1,0:T(8,128)(2,1)} %bitcast.121, f32[4,16,256,256]{2,3,1,0:T(8,128)} %get-tuple-element.18, f32[4,16,256]{2,1,0:T(8,128)S(1)} %get-tuple-element.17), kind=kOutput, calls=%fused_computation.67 | convolution fusion | flops 277348352 | bytes 18939904 | tf_op jit(solution)/shard_map/nhqk,nhqd->nhkd/dot_general | solution.py:177
  338.1 9.7 %fusion.31 = bf16[4,16,256,32]{2,3,1,0:T(8,128)(2,1)} fusion(bf16[4,3,16,256,32]{4,3,2,1,0:T(8,128)(2,1)} %bitcast.109, f32[4,16,256,256]{2,3,1,0:T(8,128)} %get-tuple-element.18, f32[4,16,256]{2,1,0:T(8,128)S(1)} %get-tuple-element.17), kind=kOutput, calls=%fused_computation.66 | convolution fusion | flops 277348352 | bytes 22085632 | tf_op jit(solution)/shard_map/nhqk,nhkd->nhqd/dot_general | solution.py:166
  347.8 3.2 copy.29
  351.0 3.2 copy.31
  354.2 3.1 copy.34
  357.2 6.0 maximum_bitcast_fusion
  363.2 16.4 %copy.35 = bf16[2,4,2,8,1,8,3,16,32]{8,7,6,5,3,2,1,0,4:T(8,128)(2,1)} copy(bf16[2,4,2,8,1,8,3,16,32]{8,5,3,1,7,2,0,6,4:T(8,128)(2,1)S(1)} %maximum_bitcast_fusion) | data formatting | bytes 6291456 | tf_op jit(solution)/shard_map/transpose | solution.py:34
  379.7 17.1 %reshape_reshape.15 = bf16[1024,1536]{1,0:T(8,128)(2,1)} reshape(bf16[2,4,2,8,1,8,3,16,32]{8,7,6,5,3,2,1,0,4:T(8,128)(2,1)} %copy.35) | data formatting | bytes 6291456 | tf_op jit(solution)/shard_map/reshape;reshape | solution.py:192
  396.7 3.1 copy.24
  399.8 10.8 %copy.25 = bf16[2,4,2,8,1,8,1,16,32]{8,7,5,3,2,1,0,6,4:T(8,128)(2,1)} copy(bf16[2,4,2,8,1,8,1,16,32]{8,5,3,1,7,2,0,6,4:T(8,128)(2,1)} %bitcast.110) | data formatting | bytes 2097152 | tf_op jit(solution)/shard_map/transpose | solution.py:34
  410.6 7.1 reshape_reshape.13
  417.7 4.2 fusion.29
  425.4 1.8 convolution_convert_fusion.1
  427.3 12.5 %collective-permute-done.24 = bf16[3,16,8,512]{3,2,1,0:T(8,128)(2,1)S(1)} collective-permute-done((bf16[3,16,8,512]{3,2,1,0:T(8,128)(2,1)S(1)}, bf16[3,16,8,512]{3,2,1,0:T(8,128)(2,1)S(1)}, u32[]{:S(2)}, u32[]{:S(2)}) %collective-permute-start.24) | collective-permute-done | bytes 393248 | tf_op jit(solution)/shard_map/ppermute | solution.py:17
  440.5 1.6 pad_maximum_fusion
  442.2 5.8 collective-permute-done.8
  448.0 10.6 %collective-permute-start.26 = (bf16[3,16,8,512]{3,2,1,0:T(8,128)(2,1)S(1)}, bf16[3,16,8,512]{3,2,1,0:T(8,128)(2,1)}, u32[]{:S(2)}, u32[]{:S(2)}) collective-permute-start(bf16[3,16,8,512]{3,2,1,0:T(8,128)(2,1)S(1)} %broadcast_select_fusion.10), channel_id=1, source_target_pairs={{2,0},{3,1},{4,2},{5,3},{6,4},{7,5},{8,6},{9,7},{10,8},{11,9},{12,... | collective-permute-start | bytes 1179656 | tf_op jit(solution)/shard_map/ppermute | solution.py:17
  462.6 77.5 %psum.15 = f32[512]{0:T(512)S(1)} all-reduce(f32[512]{0:T(512)S(1)} %get-tuple-element.5), channel_id=1, replica_groups=mesh['rad'=8,'azi'=32] {'rad','azi'}, use_global_device_ids=true, to_apply=%region_10.11 | all-reduce | flops 512 | bytes 4096 | tf_op jit(solution)/shard_map/psum | solution.py:215
  540.3 2.4 collective-permute-start.27
  543.3 18.2 %collective-permute-done.10 = bf16[3,16,8,512]{3,2,1,0:T(8,128)(2,1)S(1)} collective-permute-done((bf16[3,16,8,512]{3,2,1,0:T(8,128)(2,1)S(1)}, bf16[3,16,8,512]{3,2,1,0:T(8,128)(2,1)S(1)}, u32[]{:S(2)}, u32[]{:S(2)}) %collective-permute-start.10) | collective-permute-done | bytes 393248 | tf_op jit(solution)/shard_map/ppermute | solution.py:17
  561.5 5.3 collective-permute-start.11
  566.8 4.4 collective-permute-start.28
  571.4 30.7 %collective-permute-start.15 = (bf16[11,7,8,512]{3,2,1,0:T(8,128)(2,1)S(1)}, bf16[11,7,8,512]{3,2,1,0:T(8,128)(2,1)S(1)}, u32[]{:S(2)}, u32[]{:S(2)}) collective-permute-start(bf16[11,7,8,512]{3,2,1,0:T(8,128)(2,1)S(1)} %pad_maximum_fusion.2), channel_id=1, source_target_pairs={{31,0},{0,1},{1,2},{2,3},{3,4},{4,5},{5,6},{6,7},{7,8},{8,9},{9,10... | collective-permute-start | bytes 1892360 | tf_op jit(solution)/shard_map/ppermute | solution.py:17
  602.4 2.3 collective-permute-start.29
  604.7 22.3 %collective-permute-done.31 = bf16[11,7,8,512]{3,2,1,0:T(8,128)(2,1)S(1)} collective-permute-done((bf16[11,7,8,512]{3,2,1,0:T(8,128)(2,1)S(1)}, bf16[11,7,8,512]{3,2,1,0:T(8,128)(2,1)S(1)}, u32[]{:S(2)}, u32[]{:S(2)}) %collective-permute-start.31) | collective-permute-done | bytes 630816 | tf_op jit(solution)/shard_map/ppermute | solution.py:17
  627.5 3.5 collective-permute-start.13
  631.1 16.9 %collective-permute-start.30 = (bf16[3,16,8,512]{3,2,1,0:T(8,128)(2,1)S(1)}, bf16[3,16,8,512]{3,2,1,0:T(8,128)(2,1)S(1)}, u32[]{:S(2)}, u32[]{:S(2)}) collective-permute-start(bf16[3,16,8,512]{3,2,1,0:T(8,128)(2,1)S(1)} %broadcast_select_fusion.18), channel_id=1, source_target_pairs={{1,0},{2,1},{3,2},{4,3},{5,4},{6,5},{7,6},{8,7},{9,8},{10,9},{11,1... | collective-permute-start | bytes 1179656 | tf_op jit(solution)/shard_map/ppermute | solution.py:17
  648.5 6.1 collective-permute-start.14
  655.0 1.7 fusion.47
  656.7 3.1 collective-permute-done.14
  660.3 1.7 fusion.49
  662.0 85.3 %all-reduce.2.cloned.1.call-done = bf16[16,2048]{1,0:T(8,128)(2,1)} async-done(((bf16[16,2048]{1,0:T(8,128)(2,1)}), bf16[16,2048]{1,0:T(8,128)(2,1)}) %all-reduce.2.cloned.1.call-update) | async-done | bytes 65552 | tf_op jit(solution)/shard_map/psum | solution.py:213
  (135 shorter events, 27.0 us)
Async XLA Ops:
  7.2 18.9 %copy-start.4 = (bf16[8,16,8,512]{3,2,1,0:T(8,128)(2,1)S(1)}, bf16[8,16,8,512]{3,2,1,0:T(8,128)(2,1)}, u32[]{:S(2)}) copy-start(bf16[8,16,8,512]{3,2,1,0:T(8,128)(2,1)} %param.8) | copy-start | bytes 3145732
  7.2 218.0 %all-gather.2.cloned.1.call-start = ((), (), s32[]{:S(2)}) async-start(), calls=%async_computation.1 | async-start | bytes 1622016 | tf_op jit(solution)/shard_map/all_gather | solution.py:153
  8.3 15.1 %collective-permute-start.16 = (bf16[3,16,8,512]{3,2,1,0:T(8,128)(2,1)S(1)}, bf16[3,16,8,512]{3,2,1,0:T(8,128)(2,1)}, u32[]{:S(2)}, u32[]{:S(2)}) collective-permute-start(bf16[3,16,8,512]{3,2,1,0:T(8,128)(2,1)S(1)} %slice.93), channel_id=1, source_target_pairs={{32,0},{64,32},{96,64},{128,96},{160,128},{192,160},{224,192},{0,2... | collective-permute-start | bytes 1179656 | tf_op jit(solution)/shard_map/ppermute | solution.py:17
  14.9 15.8 %collective-permute-start = (bf16[3,16,8,512]{3,2,1,0:T(8,128)(2,1)S(1)}, bf16[3,16,8,512]{3,2,1,0:T(8,128)(2,1)S(1)}, u32[]{:S(2)}, u32[]{:S(2)}) collective-permute-start(bf16[3,16,8,512]{3,2,1,0:T(8,128)(2,1)S(1)} %slice.79), channel_id=1, source_target_pairs={{32,0},{64,32},{96,64},{128,96},{160,128},{192,160},{224,192},{0,2... | collective-permute-start | bytes 1179656 | tf_op jit(solution)/shard_map/ppermute | solution.py:17
  23.4 7.3 collective-permute-start.18
  30.7 11.5 %copy-start.12 = (bf16[3,16,8,512]{3,2,1,0:T(8,128)(2,1)}, bf16[3,16,8,512]{3,2,1,0:T(8,128)(2,1)S(1)}, u32[]{:S(2)}) copy-start(bf16[3,16,8,512]{3,2,1,0:T(8,128)(2,1)S(1)} %collective-permute-done) | copy-start | bytes 1179652
  30.7 11.5 %collective-permute-start.2 = (bf16[3,16,8,512]{3,2,1,0:T(8,128)(2,1)S(1)}, bf16[3,16,8,512]{3,2,1,0:T(8,128)(2,1)S(1)}, u32[]{:S(2)}, u32[]{:S(2)}) collective-permute-start(bf16[3,16,8,512]{3,2,1,0:T(8,128)(2,1)S(1)} %collective-permute-done), channel_id=1, source_target_pairs={{1,0},{2,1},{3,2},{4,3},{5,4},{6,5},{7,6},{8,7},{9,8},{10,9},{11,1... | collective-permute-start | bytes 1179656 | tf_op jit(solution)/shard_map/ppermute | solution.py:17
  32.1 16.4 %collective-permute-start.19 = (bf16[3,16,8,512]{3,2,1,0:T(8,128)(2,1)S(1)}, bf16[3,16,8,512]{3,2,1,0:T(8,128)(2,1)S(1)}, u32[]{:S(2)}, u32[]{:S(2)}) collective-permute-start(bf16[3,16,8,512]{3,2,1,0:T(8,128)(2,1)S(1)} %get-tuple-element.10), channel_id=1, source_target_pairs={{2,0},{3,1},{4,2},{5,3},{6,4},{7,5},{8,6},{9,7},{10,8},{11,9},{12,... | collective-permute-start | bytes 1179656 | tf_op jit(solution)/shard_map/ppermute | solution.py:17
  43.3 16.5 %copy-start.5 = (bf16[3,16,8,512]{3,2,1,0:T(8,128)(2,1)}, bf16[3,16,8,512]{3,2,1,0:T(8,128)(2,1)S(1)}, u32[]{:S(2)}) copy-start(bf16[3,16,8,512]{3,2,1,0:T(8,128)(2,1)S(1)} %get-tuple-element.12) | copy-start | bytes 1179652
  43.3 16.5 %collective-permute-start.3 = (bf16[3,16,8,512]{3,2,1,0:T(8,128)(2,1)S(1)}, bf16[3,16,8,512]{3,2,1,0:T(8,128)(2,1)}, u32[]{:S(2)}, u32[]{:S(2)}) collective-permute-start(bf16[3,16,8,512]{3,2,1,0:T(8,128)(2,1)S(1)} %get-tuple-element.12), channel_id=1, source_target_pairs={{2,0},{3,1},{4,2},{5,3},{6,4},{7,5},{8,6},{9,7},{10,8},{11,9},{12,... | collective-permute-start | bytes 1179656 | tf_op jit(solution)/shard_map/ppermute | solution.py:17
  49.3 35.1 %copy-start.14 = (bf16[16,512]{1,0:T(8,128)(2,1)S(1)}, bf16[16,512]{1,0:T(8,128)(2,1)}, u32[]{:S(2)}) copy-start(bf16[16,512]{1,0:T(8,128)(2,1)} %param.11) | copy-start | bytes 49156
  49.3 29.0 %collective-permute-start.20 = (bf16[3,16,8,512]{3,2,1,0:T(8,128)(2,1)}, bf16[3,16,8,512]{3,2,1,0:T(8,128)(2,1)}, u32[]{:S(2)}, u32[]{:S(2)}) collective-permute-start(bf16[3,16,8,512]{3,2,1,0:T(8,128)(2,1)} %broadcast_select_fusion.2), channel_id=1, source_target_pairs={{4,0},{5,1},{6,2},{7,3},{8,4},{9,5},{10,6},{11,7},{12,8},{13,9},{1... | collective-permute-start | bytes 1179656 | tf_op jit(solution)/shard_map/ppermute | solution.py:17
  58.8 601.5 %reduce-scatter.2.cloned.1.call-start = ((), (), s32[]{:S(2)}) async-start(), calls=%async_computation.2 | async-start | bytes 2162688 | tf_op jit(solution)/shard_map/reduce_scatter | solution.py:214
  59.8 105.6 %collective-permute-start.17 = (bf16[11,7,8,512]{3,2,1,0:T(8,128)(2,1)}, bf16[11,7,8,512]{3,2,1,0:T(8,128)(2,1)}, u32[]{:S(2)}, u32[]{:S(2)}) collective-permute-start(bf16[11,7,8,512]{3,2,1,0:T(8,128)(2,1)} %slice.113), channel_id=1, source_target_pairs={{1,0},{2,1},{3,2},{4,3},{5,4},{6,5},{7,6},{8,7},{9,8},{10,9},{11,1... | collective-permute-start | bytes 1892360 | tf_op jit(solution)/shard_map/ppermute | solution.py:17
  60.8 100.2 %collective-permute-start.4 = (bf16[3,16,8,512]{3,2,1,0:T(8,128)(2,1)S(1)}, bf16[3,16,8,512]{3,2,1,0:T(8,128)(2,1)}, u32[]{:S(2)}, u32[]{:S(2)}) collective-permute-start(bf16[3,16,8,512]{3,2,1,0:T(8,128)(2,1)S(1)} %broadcast_select_fusion.3), channel_id=1, source_target_pairs={{4,0},{5,1},{6,2},{7,3},{8,4},{9,5},{10,6},{11,7},{12,8},{13,9},{1... | collective-permute-start | bytes 1179656 | tf_op jit(solution)/shard_map/ppermute | solution.py:17
  80.1 82.6 %collective-permute-start.21 = (bf16[3,16,8,512]{3,2,1,0:T(8,128)(2,1)}, bf16[3,16,8,512]{3,2,1,0:T(8,128)(2,1)}, u32[]{:S(2)}, u32[]{:S(2)}) collective-permute-start(bf16[3,16,8,512]{3,2,1,0:T(8,128)(2,1)} %broadcast_select_fusion.4), channel_id=1, source_target_pairs={{8,0},{9,1},{10,2},{11,3},{12,4},{13,5},{14,6},{15,7},{16,8},{17,9... | collective-permute-start | bytes 1179656 | tf_op jit(solution)/shard_map/ppermute | solution.py:17
  160.9 36.9 %collective-permute-start.1 = (bf16[11,7,8,512]{3,2,1,0:T(8,128)(2,1)S(1)}, bf16[11,7,8,512]{3,2,1,0:T(8,128)(2,1)S(1)}, u32[]{:S(2)}, u32[]{:S(2)}) collective-permute-start(bf16[11,7,8,512]{3,2,1,0:T(8,128)(2,1)S(1)} %slice.104), channel_id=1, source_target_pairs={{1,0},{2,1},{3,2},{4,3},{5,4},{6,5},{7,6},{8,7},{9,8},{10,9},{11,1... | collective-permute-start | bytes 1892360 | tf_op jit(solution)/shard_map/ppermute | solution.py:17
  162.0 24.8 %collective-permute-start.5 = (bf16[3,16,8,512]{3,2,1,0:T(8,128)(2,1)S(1)}, bf16[3,16,8,512]{3,2,1,0:T(8,128)(2,1)S(1)}, u32[]{:S(2)}, u32[]{:S(2)}) collective-permute-start(bf16[3,16,8,512]{3,2,1,0:T(8,128)(2,1)S(1)} %broadcast_select_fusion.5), channel_id=1, source_target_pairs={{8,0},{9,1},{10,2},{11,3},{12,4},{13,5},{14,6},{15,7},{16,8},{17,9... | collective-permute-start | bytes 1179656 | tf_op jit(solution)/shard_map/ppermute | solution.py:17
  163.7 33.9 %collective-permute-start.22 = (bf16[3,16,8,512]{3,2,1,0:T(8,128)(2,1)S(1)}, bf16[3,16,8,512]{3,2,1,0:T(8,128)(2,1)S(1)}, u32[]{:S(2)}, u32[]{:S(2)}) collective-permute-start(bf16[3,16,8,512]{3,2,1,0:T(8,128)(2,1)S(1)} %broadcast_select_fusion.6), channel_id=1, source_target_pairs={{16,0},{17,1},{18,2},{19,3},{20,4},{21,5},{22,6},{23,7},{24,8},{25... | collective-permute-start | bytes 1179656 | tf_op jit(solution)/shard_map/ppermute | solution.py:17
  186.8 19.1 %collective-permute-start.6 = (bf16[3,16,8,512]{3,2,1,0:T(8,128)(2,1)S(1)}, bf16[3,16,8,512]{3,2,1,0:T(8,128)(2,1)S(1)}, u32[]{:S(2)}, u32[]{:S(2)}) collective-permute-start(bf16[3,16,8,512]{3,2,1,0:T(8,128)(2,1)S(1)} %broadcast_select_fusion.7), channel_id=1, source_target_pairs={{16,0},{17,1},{18,2},{19,3},{20,4},{21,5},{22,6},{23,7},{24,8},{25... | collective-permute-start | bytes 1179656 | tf_op jit(solution)/shard_map/ppermute | solution.py:17
  197.7 8.4 %collective-permute-start.23 = (bf16[3,16,8,512]{3,2,1,0:T(8,128)(2,1)S(1)}, bf16[3,16,8,512]{3,2,1,0:T(8,128)(2,1)S(1)}, u32[]{:S(2)}, u32[]{:S(2)}) collective-permute-start(bf16[3,16,8,512]{3,2,1,0:T(8,128)(2,1)S(1)} %broadcast_select_fusion.8), channel_id=1, source_target_pairs={{1,0},{2,1},{3,2},{4,3},{5,4},{6,5},{7,6},{8,7},{9,8},{10,9},{11,1... | collective-permute-start | bytes 1179656 | tf_op jit(solution)/shard_map/ppermute | solution.py:17
  206.0 15.3 %collective-permute-start.7 = (bf16[3,16,8,512]{3,2,1,0:T(8,128)(2,1)S(1)}, bf16[3,16,8,512]{3,2,1,0:T(8,128)(2,1)S(1)}, u32[]{:S(2)}, u32[]{:S(2)}) collective-permute-start(bf16[3,16,8,512]{3,2,1,0:T(8,128)(2,1)S(1)} %broadcast_select_fusion.9), channel_id=1, source_target_pairs={{1,0},{2,1},{3,2},{4,3},{5,4},{6,5},{7,6},{8,7},{9,8},{10,9},{11,1... | collective-permute-start | bytes 1179656 | tf_op jit(solution)/shard_map/ppermute | solution.py:17
  206.3 2.1 copy-start.10
  207.4 1.0 copy-start.1
  221.8 1.6 copy-start.13
  314.8 3.3 copy-start
  351.0 3.2 copy-start.8
  379.7 17.1 %copy-start.7 = (bf16[4,16,256,32]{2,3,1,0:T(8,128)(2,1)S(1)}, bf16[4,16,256,32]{2,3,1,0:T(8,128)(2,1)}, u32[]{:S(2)}) copy-start(bf16[4,16,256,32]{2,3,1,0:T(8,128)(2,1)} %fusion.31) | copy-start | bytes 3145732
  410.6 7.1 copy-start.15
  417.7 4.2 copy-start.2
  421.9 1.3 copy-start.6
  421.9 1.3 copy-start.11
  423.1 2.0 copy-start.3
  423.1 2.4 copy-start.9
  423.1 16.7 %collective-permute-start.24 = (bf16[3,16,8,512]{3,2,1,0:T(8,128)(2,1)S(1)}, bf16[3,16,8,512]{3,2,1,0:T(8,128)(2,1)S(1)}, u32[]{:S(2)}, u32[]{:S(2)}) collective-permute-start(bf16[3,16,8,512]{3,2,1,0:T(8,128)(2,1)S(1)} %bitcast.123), channel_id=1, source_target_pairs={{224,0},{0,32},{32,64},{64,96},{96,128},{128,160},{160,192},{192,2... | collective-permute-start | bytes 1179656 | tf_op jit(solution)/shard_map/ppermute | solution.py:17
  424.8 23.2 %collective-permute-start.8 = (bf16[3,16,8,512]{3,2,1,0:T(8,128)(2,1)}, bf16[3,16,8,512]{3,2,1,0:T(8,128)(2,1)S(1)}, u32[]{:S(2)}, u32[]{:S(2)}) collective-permute-start(bf16[3,16,8,512]{3,2,1,0:T(8,128)(2,1)} %bitcast.13), channel_id=1, source_target_pairs={{224,0},{0,32},{32,64},{64,96},{96,128},{128,160},{160,192},{192,2... | collective-permute-start | bytes 1179656 | tf_op jit(solution)/shard_map/ppermute | solution.py:17
  439.7 8.2 %collective-permute-start.25 = (bf16[3,16,8,512]{3,2,1,0:T(8,128)(2,1)S(1)}, bf16[3,16,8,512]{3,2,1,0:T(8,128)(2,1)}, u32[]{:S(2)}, u32[]{:S(2)}) collective-permute-start(bf16[3,16,8,512]{3,2,1,0:T(8,128)(2,1)S(1)} %collective-permute-done.24), channel_id=1, source_target_pairs={{1,0},{2,1},{3,2},{4,3},{5,4},{6,5},{7,6},{8,7},{9,8},{10,9},{11,1... | collective-permute-start | bytes 1179656 | tf_op jit(solution)/shard_map/ppermute | solution.py:17
  442.1 305.2 %all-reduce.2.cloned.1.call-start = ((), (), s32[]{:S(2)}) async-start(), calls=%async_computation.3 | async-start | bytes 131072 | tf_op jit(solution)/shard_map/psum | solution.py:213
  448.0 92.1 %collective-permute-start.9 = (bf16[3,16,8,512]{3,2,1,0:T(8,128)(2,1)S(1)}, bf16[3,16,8,512]{3,2,1,0:T(8,128)(2,1)}, u32[]{:S(2)}, u32[]{:S(2)}) collective-permute-start(bf16[3,16,8,512]{3,2,1,0:T(8,128)(2,1)S(1)} %collective-permute-done.8), channel_id=1, source_target_pairs={{1,0},{2,1},{3,2},{4,3},{5,4},{6,5},{7,6},{8,7},{9,8},{10,9},{11,1... | collective-permute-start | bytes 1179656 | tf_op jit(solution)/shard_map/ppermute | solution.py:17
  448.0 92.2 %collective-permute-start.26 = (bf16[3,16,8,512]{3,2,1,0:T(8,128)(2,1)S(1)}, bf16[3,16,8,512]{3,2,1,0:T(8,128)(2,1)}, u32[]{:S(2)}, u32[]{:S(2)}) collective-permute-start(bf16[3,16,8,512]{3,2,1,0:T(8,128)(2,1)S(1)} %broadcast_select_fusion.10), channel_id=1, source_target_pairs={{2,0},{3,1},{4,2},{5,3},{6,4},{7,5},{8,6},{9,7},{10,8},{11,9},{12,... | collective-permute-start | bytes 1179656 | tf_op jit(solution)/shard_map/ppermute | solution.py:17
  540.1 21.4 %collective-permute-start.10 = (bf16[3,16,8,512]{3,2,1,0:T(8,128)(2,1)S(1)}, bf16[3,16,8,512]{3,2,1,0:T(8,128)(2,1)S(1)}, u32[]{:S(2)}, u32[]{:S(2)}) collective-permute-start(bf16[3,16,8,512]{3,2,1,0:T(8,128)(2,1)S(1)} %broadcast_select_fusion.11), channel_id=1, source_target_pairs={{2,0},{3,1},{4,2},{5,3},{6,4},{7,5},{8,6},{9,7},{10,8},{11,9},{12,... | collective-permute-start | bytes 1179656 | tf_op jit(solution)/shard_map/ppermute | solution.py:17
  540.3 26.5 %collective-permute-start.27 = (bf16[3,16,8,512]{3,2,1,0:T(8,128)(2,1)S(1)}, bf16[3,16,8,512]{3,2,1,0:T(8,128)(2,1)S(1)}, u32[]{:S(2)}, u32[]{:S(2)}) collective-permute-start(bf16[3,16,8,512]{3,2,1,0:T(8,128)(2,1)S(1)} %broadcast_select_fusion.12), channel_id=1, source_target_pairs={{4,0},{5,1},{6,2},{7,3},{8,4},{9,5},{10,6},{11,7},{12,8},{13,9},{1... | collective-permute-start | bytes 1179656 | tf_op jit(solution)/shard_map/ppermute | solution.py:17
  561.5 40.6 %collective-permute-start.11 = (bf16[3,16,8,512]{3,2,1,0:T(8,128)(2,1)S(1)}, bf16[3,16,8,512]{3,2,1,0:T(8,128)(2,1)S(1)}, u32[]{:S(2)}, u32[]{:S(2)}) collective-permute-start(bf16[3,16,8,512]{3,2,1,0:T(8,128)(2,1)S(1)} %broadcast_select_fusion.13), channel_id=1, source_target_pairs={{4,0},{5,1},{6,2},{7,3},{8,4},{9,5},{10,6},{11,7},{12,8},{13,9},{1... | collective-permute-start | bytes 1179656 | tf_op jit(solution)/shard_map/ppermute | solution.py:17
  566.8 35.5 %collective-permute-start.28 = (bf16[3,16,8,512]{3,2,1,0:T(8,128)(2,1)S(1)}, bf16[3,16,8,512]{3,2,1,0:T(8,128)(2,1)S(1)}, u32[]{:S(2)}, u32[]{:S(2)}) collective-permute-start(bf16[3,16,8,512]{3,2,1,0:T(8,128)(2,1)S(1)} %broadcast_select_fusion.14), channel_id=1, source_target_pairs={{8,0},{9,1},{10,2},{11,3},{12,4},{13,5},{14,6},{15,7},{16,8},{17,9... | collective-permute-start | bytes 1179656 | tf_op jit(solution)/shard_map/ppermute | solution.py:17
  571.3 55.7 %collective-permute-start.31 = (bf16[11,7,8,512]{3,2,1,0:T(8,128)(2,1)S(1)}, bf16[11,7,8,512]{3,2,1,0:T(8,128)(2,1)S(1)}, u32[]{:S(2)}, u32[]{:S(2)}) collective-permute-start(bf16[11,7,8,512]{3,2,1,0:T(8,128)(2,1)S(1)} %pad_maximum_fusion.1), channel_id=1, source_target_pairs={{31,0},{0,1},{1,2},{2,3},{3,4},{4,5},{5,6},{6,7},{7,8},{8,9},{9,10... | collective-permute-start | bytes 1892360 | tf_op jit(solution)/shard_map/ppermute | solution.py:17
  571.4 76.5 %collective-permute-start.15 = (bf16[11,7,8,512]{3,2,1,0:T(8,128)(2,1)S(1)}, bf16[11,7,8,512]{3,2,1,0:T(8,128)(2,1)S(1)}, u32[]{:S(2)}, u32[]{:S(2)}) collective-permute-start(bf16[11,7,8,512]{3,2,1,0:T(8,128)(2,1)S(1)} %pad_maximum_fusion.2), channel_id=1, source_target_pairs={{31,0},{0,1},{1,2},{2,3},{3,4},{4,5},{5,6},{6,7},{7,8},{8,9},{9,10... | collective-permute-start | bytes 1892360 | tf_op jit(solution)/shard_map/ppermute | solution.py:17
  602.2 25.2 %collective-permute-start.12 = (bf16[3,16,8,512]{3,2,1,0:T(8,128)(2,1)S(1)}, bf16[3,16,8,512]{3,2,1,0:T(8,128)(2,1)S(1)}, u32[]{:S(2)}, u32[]{:S(2)}) collective-permute-start(bf16[3,16,8,512]{3,2,1,0:T(8,128)(2,1)S(1)} %broadcast_select_fusion.15), channel_id=1, source_target_pairs={{8,0},{9,1},{10,2},{11,3},{12,4},{13,5},{14,6},{15,7},{16,8},{17,9... | collective-permute-start | bytes 1179656 | tf_op jit(solution)/shard_map/ppermute | solution.py:17
  602.4 28.6 %collective-permute-start.29 = (bf16[3,16,8,512]{3,2,1,0:T(8,128)(2,1)S(1)}, bf16[3,16,8,512]{3,2,1,0:T(8,128)(2,1)S(1)}, u32[]{:S(2)}, u32[]{:S(2)}) collective-permute-start(bf16[3,16,8,512]{3,2,1,0:T(8,128)(2,1)S(1)} %broadcast_select_fusion.16), channel_id=1, source_target_pairs={{16,0},{17,1},{18,2},{19,3},{20,4},{21,5},{22,6},{23,7},{24,8},{25... | collective-permute-start | bytes 1179656 | tf_op jit(solution)/shard_map/ppermute | solution.py:17
  627.5 21.0 %collective-permute-start.13 = (bf16[3,16,8,512]{3,2,1,0:T(8,128)(2,1)S(1)}, bf16[3,16,8,512]{3,2,1,0:T(8,128)(2,1)S(1)}, u32[]{:S(2)}, u32[]{:S(2)}) collective-permute-start(bf16[3,16,8,512]{3,2,1,0:T(8,128)(2,1)S(1)} %broadcast_select_fusion.17), channel_id=1, source_target_pairs={{16,0},{17,1},{18,2},{19,3},{20,4},{21,5},{22,6},{23,7},{24,8},{25... | collective-permute-start | bytes 1179656 | tf_op jit(solution)/shard_map/ppermute | solution.py:17
  631.1 23.5 %collective-permute-start.30 = (bf16[3,16,8,512]{3,2,1,0:T(8,128)(2,1)S(1)}, bf16[3,16,8,512]{3,2,1,0:T(8,128)(2,1)S(1)}, u32[]{:S(2)}, u32[]{:S(2)}) collective-permute-start(bf16[3,16,8,512]{3,2,1,0:T(8,128)(2,1)S(1)} %broadcast_select_fusion.18), channel_id=1, source_target_pairs={{1,0},{2,1},{3,2},{4,3},{5,4},{6,5},{7,6},{8,7},{9,8},{10,9},{11,1... | collective-permute-start | bytes 1179656 | tf_op jit(solution)/shard_map/ppermute | solution.py:17
  648.5 11.4 %collective-permute-start.14 = (bf16[3,16,8,512]{3,2,1,0:T(8,128)(2,1)S(1)}, bf16[3,16,8,512]{3,2,1,0:T(8,128)(2,1)S(1)}, u32[]{:S(2)}, u32[]{:S(2)}) collective-permute-start(bf16[3,16,8,512]{3,2,1,0:T(8,128)(2,1)S(1)} %broadcast_select_fusion.19), channel_id=1, source_target_pairs={{1,0},{2,1},{3,2},{4,3},{5,4},{6,5},{7,6},{8,7},{9,8},{10,9},{11,1... | collective-permute-start | bytes 1179656 | tf_op jit(solution)/shard_map/ppermute | solution.py:17
Sparse Core Ops, SparseCore 0:
  58.9 71.1 all-gather.1
  442.3 115.6 reduce-scatter.1
  660.4 86.8 all-reduce.1
where the time goes:
time: 767 us; the launch traced here: 756 us
  waiting for transfers between devices  195 us (25%)
  blocking collectives  148 us (19%)
  starting transfers between devices  140 us (18%)
  local copies, waits for them, and re-layouts  114 us (15%)
  matrix products  69.8 us (9%)
  other arithmetic  63.6 us (8%)
  between operations  25.9 us (3%)
    ppermute x32, starting transfers between devices, shifted_2(): return lax.ppermute(block, axis, route)  140 us
    ppermute x32, waiting for transfers between devices, shifted_2(): return lax.ppermute(block, axis, route)  109 us
    psum x1, waiting for transfers between devices, on_device(): lax.psum(jnp.concatenate([term_qkv, term_out], axis=1).astype(jnp.bfloat1...  85.3 us
    psum x1, blocking collectives, on_device(): gain_total = lax.psum(jnp.sum(d_hidden * normed, axis=0), ('rad', 'azi'))  77.5 us
    all_gather x1, blocking collectives, on_device(): lax.all_gather(out_weight, 'azi', axis=0, tiled=True)  70.5 us
    another operation x4, local copies, waits for them, and re-layouts, to_windows(): tensor.reshape(extent_r // WR, WR, extent_a // WA, WA, extent_z // WZ, WZ...  38.5 us
    transpose x2, local copies, waits for them, and re-layouts, from_windows(): windows = windows.transpose(0, 5, 1, 6, 2, 7, 3, 4, 8)  27.3 us
    sub x1, other arithmetic, on_device(): weights = jax.nn.softmax(scores, axis=-1)  19.6 us
  transfers between devices with their start and end apart: 35, of which 12 were waited for; matrix products, arithmetic and copies ran while one was open for 6% of the time, Pallas kernels for 0%

commit v1 on v0

--- a/solution.py
+++ b/solution.py
@@ -212,7 +212,7 @@
     term_out = lax.dot_general(attended, grad_low, contract, preferred_element_type=jnp.float32)
     whole_term = lax.psum(jnp.concatenate([term_qkv, term_out], axis=1).astype(jnp.bfloat16), "rad")
     share = lax.psum_scatter(whole_term, "azi", scatter_dimension=0, tiled=True).astype(jnp.float32)
-    gain_total = lax.psum(jnp.sum(d_hidden * normed, axis=0), ("rad", "azi"))
+    gain_total = jnp.sum(lax.all_gather(jnp.sum(d_hidden * normed, axis=0), ("rad", "azi")), axis=0)
     factor = float(number * n_rad * n_azi) ** (-0.5)
     grad_qkv = share[:, : 3 * width] * factor
     grad_out = share[:, 3 * width :] * factor

time: 767 us -> 1030 us (1.34)
  blocking collectives: 148 us -> 415 us
  starting transfers between devices: 140 us -> 77.2 us
  waiting for transfers between devices: 195 us -> 251 us
    all_gather x0 -> x1, blocking collectives: none -> 345 us  [on_device(): lax.all_gather(jnp.sum(d_hidden * normed, axis=0), ('rad', 'azi'))]
    psum x1 -> x0, blocking collectives: 77.5 us -> none  [on_device(): gain_total = lax.psum(jnp.sum(d_hidden * normed, axis=0), ('rad', 'azi'))]
    ppermute x32, starting transfers between devices: 140 us -> 77.1 us  [shifted_2(): return lax.ppermute(block, axis, route)]
    ppermute x32, waiting for transfers between devices: 109 us -> 141 us  [shifted_2(): return lax.ppermute(block, axis, route)]
    psum x1, waiting for transfers between devices: 85.3 us -> 110 us  [on_device(): lax.psum(jnp.concatenate([term_qkv, term_out], axis=1).astype(jnp.bfloat1...]
  transfers between devices with their start and end apart: 35 -> 35, of which waited for: 12 -> 17; matrix products, arithmetic and copies ran while one was open for 6% -> 5% of each run, Pallas kernels for 0% -> 0%
where the time goes in v1:
time: 1030 us; the launch traced here: 1020 us
  blocking collectives  415 us (40%)
  waiting for transfers between devices  251 us (24%)
  local copies, waits for them, and re-layouts  114 us (11%)
  starting transfers between devices  77.2 us (7%)
  matrix products  69.8 us (7%)
  other arithmetic  65.7 us (6%)
  between operations  26 us (3%)
    all_gather x1, blocking collectives, on_device(): lax.all_gather(jnp.sum(d_hidden * normed, axis=0), ('rad', 'azi'))  345 us
    ppermute x32, waiting for transfers between devices, shifted_2(): return lax.ppermute(block, axis, route)  141 us
    psum x1, waiting for transfers between devices, on_device(): lax.psum(jnp.concatenate([term_qkv, term_out], axis=1).astype(jnp.bfloat1...  110 us
    ppermute x32, starting transfers between devices, shifted_2(): return lax.ppermute(block, axis, route)  77.1 us
    all_gather x1, blocking collectives, on_device(): lax.all_gather(out_weight, 'azi', axis=0, tiled=True)  70.5 us
    another operation x4, local copies, waits for them, and re-layouts, to_windows(): tensor.reshape(extent_r // WR, WR, extent_a // WA, WA, extent_z // WZ, WZ...  38.5 us
    transpose x2, local copies, waits for them, and re-layouts, from_windows(): windows = windows.transpose(0, 5, 1, 6, 2, 7, 3, 4, 8)  27.3 us
  transfers between devices with their start and end apart: 35, of which 17 were waited for; matrix products, arithmetic and copies ran while one was open for 5% of the time, Pallas kernels for 0%

profile of v1, /device:TPU:32, one launch (start us, length us, event | category | flops | bytes accessed | tf_op | source)
XLA Modules:
  0.0 1019.5 jit_solution(1208263721121899287)
XLA Ops:
  8.3 5.6 collective-permute-start.16
  15.7 7.7 collective-permute-done.16
  24.0 1.4 fusion.61
  26.2 4.5 collective-permute-done
  30.7 1.4 broadcast_select_fusion
  32.1 8.7 collective-permute-start.19
  40.8 1.3 constant_dynamic-update-slice_fusion.1
  43.3 4.6 collective-permute-start.3
  49.3 9.5 collective-permute-start.20
  60.8 10.2 %collective-permute-start.4 = (bf16[3,16,8,512]{3,2,1,0:T(8,128)(2,1)S(1)}, bf16[3,16,8,512]{3,2,1,0:T(8,128)(2,1)}, u32[]{:S(2)}, u32[]{:S(2)}) collective-permute-start(bf16[3,16,8,512]{3,2,1,0:T(8,128)(2,1)S(1)} %broadcast_select_fusion.3), channel_id=1, source_target_pairs={{4,0},{5,1},{6,2},{7,3},{8,4},{9,5},{10,6},{11,7},{12,8},{13,9},{1... | collective-permute-start | bytes 1179656 | tf_op jit(solution)/shard_map/ppermute | solution.py:17
  71.0 7.3 collective-permute-done.20
  78.3 1.8 broadcast_select_fusion.4
  80.1 4.3 collective-permute-start.21
  84.4 70.5 %all_gather.13 = bf16[512,512]{1,0:T(8,128)(2,1)} all-gather(bf16[16,512]{1,0:T(8,128)(2,1)S(1)} %copy-done.14), channel_id=1, replica_groups=mesh['rad'=8,'azi'=32] {'azi'}, dimensions={0}, use_global_device_ids=true | all-gather | bytes 540672 | tf_op jit(solution)/shard_map/all_gather | solution.py:154
  167.6 1.7 collective-permute-start.22
  169.3 1.5 fusion.39
  170.8 19.8 %collective-permute-done.5 = bf16[3,16,8,512]{3,2,1,0:T(8,128)(2,1)S(1)} collective-permute-done((bf16[3,16,8,512]{3,2,1,0:T(8,128)(2,1)S(1)}, bf16[3,16,8,512]{3,2,1,0:T(8,128)(2,1)S(1)}, u32[]{:S(2)}, u32[]{:S(2)}) %collective-permute-start.5) | collective-permute-done | bytes 393248 | tf_op jit(solution)/shard_map/ppermute | solution.py:17
  192.1 7.7 collective-permute-done.6
  202.2 1.7 convolution_convert_fusion.2
  203.9 5.9 reshape_reshape.14
  209.8 5.3 copy.44
  217.6 1.4 fusion.17
  219.0 4.8 convolution_convert_fusion
  223.9 14.6 %reshape_reshape.12 = bf16[2,4,2,8,1,8,3,16,32]{8,7,6,5,3,2,1,0,4:T(8,128)(2,1)} reshape(bf16[1024,1536]{1,0:T(8,128)(2,1)} %convolution_convert_fusion) | data formatting | bytes 6291456 | tf_op jit(solution)/shard_map/reshape;reshape | solution.py:22
  238.5 12.8 %copy.37 = bf16[2,4,2,8,1,8,3,16,32]{8,5,3,1,7,6,2,0,4:T(8,128)(2,1)} copy(bf16[2,4,2,8,1,8,3,16,32]{8,7,6,5,3,2,1,0,4:T(8,128)(2,1)} %reshape_reshape.12) | data formatting | bytes 6291456 | tf_op jit(solution)/shard_map/reshape;reshape | solution.py:22
  251.2 11.6 %fusion.11 = f32[4,16,256,256]{2,3,1,0:T(8,128)} fusion(bf16[4,3,16,256,32]{4,3,2,1,0:T(8,128)(2,1)} %bitcast.106), kind=kOutput, calls=%fused_computation.19 | convolution fusion | flops 268435456 | bytes 25165824 | tf_op jit(solution)/shard_map/nhqd,nhkd->nhqk/dot_general | solution.py:161
  262.8 19.6 %fusion.62 = (f32[4,16,256]{2,1,0:T(8,128)S(1)}, f32[4,16,256,256]{2,3,1,0:T(8,128)}) fusion(f32[4,16,256,256]{2,3,1,0:T(8,128)} %fusion.11), kind=kOutput, calls=%fused_computation.143 | output fusion | flops 16777472 | bytes 33619968 | tf_op jit(solution)/shard_map/sub | solution.py:164
  282.4 14.5 %multiply_reduce_fusion = (f32[4,16,256]{2,1,0:T(8,128)S(1)}, f32[4,16,256,256]{2,3,1,0:T(8,128)}) fusion(f32[4,16,256,256]{2,3,1,0:T(8,128)} %get-tuple-element.18, f32[4,16,256]{2,1,0:T(8,128)S(1)} %get-tuple-element.17, bf16[4,16,256,32]{3,2,1,0:T(8,128)(2,1)} %bitcast.121, bf16[4,3,16,256,32]{4,3,2,1,0:T(8,128)(2,1)} %bitcast.107), kind=kOutput, calls=%fused_computation.2 | convolution fusion | flops 281001984 | bytes 42074112 | tf_op jit(solution)/shard_map/nhqd,nhkd->nhqk/dot_general | solution.py:176
  296.9 11.7 %multiply_convert_fusion = bf16[4,16,256,256]{2,3,1,0:T(8,128)(2,1)S(1)} fusion(f32[4,16,256,256]{2,3,1,0:T(8,128)} %get-tuple-element.20, f32[4,16,256]{2,1,0:T(8,128)S(1)} %get-tuple-element.19, f32[4,16,256,256]{2,3,1,0:T(8,128)} %get-tuple-element.18, f32[4,16,256]{2,1,0:T(8,128)S(1)} %get-tuple-element.17), kind=kLoop, calls=%fused_computation.1 | loop fusion | flops 16777216 | bytes 42074112 | tf_op jit(solution)/shard_map/convert_element_type | solution.py:182
  308.6 3.3 copy-done
  311.9 3.7 multiply_convert_fusion.2
  315.6 7.1 multiply_convert_fusion.1
  322.7 9.3 fusion.34
  332.0 9.7 fusion.31
  341.6 3.2 copy.47
  344.8 3.2 copy.49
  348.0 3.1 copy.52
  351.1 6.0 maximum_bitcast_fusion
  357.1 16.4 %copy.53 = bf16[2,4,2,8,1,8,3,16,32]{8,7,6,5,3,2,1,0,4:T(8,128)(2,1)} copy(bf16[2,4,2,8,1,8,3,16,32]{8,5,3,1,7,2,0,6,4:T(8,128)(2,1)S(1)} %maximum_bitcast_fusion) | data formatting | bytes 6291456 | tf_op jit(solution)/shard_map/transpose | solution.py:34
  373.5 17.1 %reshape_reshape.15 = bf16[1024,1536]{1,0:T(8,128)(2,1)} reshape(bf16[2,4,2,8,1,8,3,16,32]{8,7,6,5,3,2,1,0,4:T(8,128)(2,1)} %copy.53) | data formatting | bytes 6291456 | tf_op jit(solution)/shard_map/reshape;reshape | solution.py:192
  390.6 3.1 copy.42
  393.6 10.8 %copy.43 = bf16[2,4,2,8,1,8,1,16,32]{8,7,5,3,2,1,0,6,4:T(8,128)(2,1)} copy(bf16[2,4,2,8,1,8,1,16,32]{8,5,3,1,7,2,0,6,4:T(8,128)(2,1)} %bitcast.111) | data formatting | bytes 2097152 | tf_op jit(solution)/shard_map/transpose | solution.py:34
  404.5 7.1 reshape_reshape.13
  411.6 4.2 fusion.29
  419.3 1.8 convolution_convert_fusion.1
  421.1 12.5 %collective-permute-done.24 = bf16[3,16,8,512]{3,2,1,0:T(8,128)(2,1)S(1)} collective-permute-done((bf16[3,16,8,512]{3,2,1,0:T(8,128)(2,1)S(1)}, bf16[3,16,8,512]{3,2,1,0:T(8,128)(2,1)S(1)}, u32[]{:S(2)}, u32[]{:S(2)}) %collective-permute-start.24) | collective-permute-done | bytes 393248 | tf_op jit(solution)/shard_map/ppermute | solution.py:17
  434.3 1.6 pad_maximum_fusion
  436.0 5.7 collective-permute-done.8
  442.5 12.7 %collective-permute-start.26 = (bf16[3,16,8,512]{3,2,1,0:T(8,128)(2,1)}, bf16[3,16,8,512]{3,2,1,0:T(8,128)(2,1)}, u32[]{:S(2)}, u32[]{:S(2)}) collective-permute-start(bf16[3,16,8,512]{3,2,1,0:T(8,128)(2,1)} %broadcast_select_fusion.10), channel_id=1, source_target_pairs={{2,0},{3,1},{4,2},{5,3},{6,4},{7,5},{8,6},{9,7},{10,8},{11,9},{12,... | collective-permute-start | bytes 1179656 | tf_op jit(solution)/shard_map/ppermute | solution.py:17
  455.2 344.7 %all-gather.1 = f32[256,1,512]{2,1,0:T(1,128)S(1)} all-gather(f32[1,1,512]{2,1,0:T(1,128)S(1)} %bitcast.125), channel_id=2, replica_groups=mesh['rad'=8,'azi'=32] {'rad','azi'}, dimensions={0}, use_global_device_ids=true | all-gather | bytes 526336 | tf_op jit(solution)/shard_map/all_gather | solution.py:215
  800.3 8.1 collective-permute-start.10
  810.1 15.8 %collective-permute-done.10 = bf16[3,16,8,512]{3,2,1,0:T(8,128)(2,1)S(1)} collective-permute-done((bf16[3,16,8,512]{3,2,1,0:T(8,128)(2,1)S(1)}, bf16[3,16,8,512]{3,2,1,0:T(8,128)(2,1)S(1)}, u32[]{:S(2)}, u32[]{:S(2)}) %collective-permute-start.10) | collective-permute-done | bytes 393248 | tf_op jit(solution)/shard_map/ppermute | solution.py:17
  826.1 14.2 %collective-permute-done.27 = bf16[3,16,8,512]{3,2,1,0:T(8,128)(2,1)S(1)} collective-permute-done((bf16[3,16,8,512]{3,2,1,0:T(8,128)(2,1)S(1)}, bf16[3,16,8,512]{3,2,1,0:T(8,128)(2,1)S(1)}, u32[]{:S(2)}, u32[]{:S(2)}) %collective-permute-start.27) | collective-permute-done | bytes 393248 | tf_op jit(solution)/shard_map/ppermute | solution.py:17
  840.7 19.5 %collective-permute-done.11 = bf16[3,16,8,512]{3,2,1,0:T(8,128)(2,1)S(1)} collective-permute-done((bf16[3,16,8,512]{3,2,1,0:T(8,128)(2,1)S(1)}, bf16[3,16,8,512]{3,2,1,0:T(8,128)(2,1)S(1)}, u32[]{:S(2)}, u32[]{:S(2)}) %collective-permute-start.11) | collective-permute-done | bytes 393248 | tf_op jit(solution)/shard_map/ppermute | solution.py:17
  860.3 9.4 collective-permute-done.28
  870.4 7.7 collective-permute-done.12
  878.2 2.5 collective-permute-done.29
  880.8 4.6 collective-permute-start.30
  885.8 3.3 collective-permute-done.13
  889.2 3.9 collective-permute-start.14
  893.5 1.7 fusion.47
  895.3 3.1 collective-permute-done.14
  898.9 1.7 fusion.49
  900.6 109.8 %all-reduce.2.cloned.1.call-done = bf16[16,2048]{1,0:T(8,128)(2,1)} async-done(((bf16[16,2048]{1,0:T(8,128)(2,1)}), bf16[16,2048]{1,0:T(8,128)(2,1)}) %all-reduce.2.cloned.1.call-update) | async-done | bytes 65552 | tf_op jit(solution)/shard_map/psum | solution.py:213
  (136 shorter events, 28.9 us)
Async XLA Ops:
  7.2 18.9 %copy-start.4 = (bf16[8,16,8,512]{3,2,1,0:T(8,128)(2,1)S(1)}, bf16[8,16,8,512]{3,2,1,0:T(8,128)(2,1)}, u32[]{:S(2)}) copy-start(bf16[8,16,8,512]{3,2,1,0:T(8,128)(2,1)} %param.8) | copy-start | bytes 3145732
  7.2 211.9 %all-gather.4.cloned.1.call-start = ((), (), s32[]{:S(2)}) async-start(), calls=%async_computation.1 | async-start | bytes 1622016 | tf_op jit(solution)/shard_map/all_gather | solution.py:153
  8.3 15.1 %collective-permute-start.16 = (bf16[3,16,8,512]{3,2,1,0:T(8,128)(2,1)S(1)}, bf16[3,16,8,512]{3,2,1,0:T(8,128)(2,1)}, u32[]{:S(2)}, u32[]{:S(2)}) collective-permute-start(bf16[3,16,8,512]{3,2,1,0:T(8,128)(2,1)S(1)} %slice.93), channel_id=1, source_target_pairs={{32,0},{64,32},{96,64},{128,96},{160,128},{192,160},{224,192},{0,2... | collective-permute-start | bytes 1179656 | tf_op jit(solution)/shard_map/ppermute | solution.py:17
  14.9 15.8 %collective-permute-start = (bf16[3,16,8,512]{3,2,1,0:T(8,128)(2,1)S(1)}, bf16[3,16,8,512]{3,2,1,0:T(8,128)(2,1)S(1)}, u32[]{:S(2)}, u32[]{:S(2)}) collective-permute-start(bf16[3,16,8,512]{3,2,1,0:T(8,128)(2,1)S(1)} %slice.79), channel_id=1, source_target_pairs={{32,0},{64,32},{96,64},{128,96},{160,128},{192,160},{224,192},{0,2... | collective-permute-start | bytes 1179656 | tf_op jit(solution)/shard_map/ppermute | solution.py:17
  23.4 7.3 collective-permute-start.18
  30.7 11.5 %copy-start.12 = (bf16[3,16,8,512]{3,2,1,0:T(8,128)(2,1)}, bf16[3,16,8,512]{3,2,1,0:T(8,128)(2,1)S(1)}, u32[]{:S(2)}) copy-start(bf16[3,16,8,512]{3,2,1,0:T(8,128)(2,1)S(1)} %collective-permute-done) | copy-start | bytes 1179652
  30.7 11.5 %collective-permute-start.2 = (bf16[3,16,8,512]{3,2,1,0:T(8,128)(2,1)S(1)}, bf16[3,16,8,512]{3,2,1,0:T(8,128)(2,1)S(1)}, u32[]{:S(2)}, u32[]{:S(2)}) collective-permute-start(bf16[3,16,8,512]{3,2,1,0:T(8,128)(2,1)S(1)} %collective-permute-done), channel_id=1, source_target_pairs={{1,0},{2,1},{3,2},{4,3},{5,4},{6,5},{7,6},{8,7},{9,8},{10,9},{11,1... | collective-permute-start | bytes 1179656 | tf_op jit(solution)/shard_map/ppermute | solution.py:17
  32.1 16.4 %collective-permute-start.19 = (bf16[3,16,8,512]{3,2,1,0:T(8,128)(2,1)S(1)}, bf16[3,16,8,512]{3,2,1,0:T(8,128)(2,1)S(1)}, u32[]{:S(2)}, u32[]{:S(2)}) collective-permute-start(bf16[3,16,8,512]{3,2,1,0:T(8,128)(2,1)S(1)} %get-tuple-element.10), channel_id=1, source_target_pairs={{2,0},{3,1},{4,2},{5,3},{6,4},{7,5},{8,6},{9,7},{10,8},{11,9},{12,... | collective-permute-start | bytes 1179656 | tf_op jit(solution)/shard_map/ppermute | solution.py:17
  43.3 16.5 %copy-start.5 = (bf16[3,16,8,512]{3,2,1,0:T(8,128)(2,1)}, bf16[3,16,8,512]{3,2,1,0:T(8,128)(2,1)S(1)}, u32[]{:S(2)}) copy-start(bf16[3,16,8,512]{3,2,1,0:T(8,128)(2,1)S(1)} %get-tuple-element.12) | copy-start | bytes 1179652
  43.3 16.5 %collective-permute-start.3 = (bf16[3,16,8,512]{3,2,1,0:T(8,128)(2,1)S(1)}, bf16[3,16,8,512]{3,2,1,0:T(8,128)(2,1)}, u32[]{:S(2)}, u32[]{:S(2)}) collective-permute-start(bf16[3,16,8,512]{3,2,1,0:T(8,128)(2,1)S(1)} %get-tuple-element.12), channel_id=1, source_target_pairs={{2,0},{3,1},{4,2},{5,3},{6,4},{7,5},{8,6},{9,7},{10,8},{11,9},{12,... | collective-permute-start | bytes 1179656 | tf_op jit(solution)/shard_map/ppermute | solution.py:17
  49.3 35.1 %copy-start.14 = (bf16[16,512]{1,0:T(8,128)(2,1)S(1)}, bf16[16,512]{1,0:T(8,128)(2,1)}, u32[]{:S(2)}) copy-start(bf16[16,512]{1,0:T(8,128)(2,1)} %param.11) | copy-start | bytes 49156
  49.3 29.0 %collective-permute-start.20 = (bf16[3,16,8,512]{3,2,1,0:T(8,128)(2,1)}, bf16[3,16,8,512]{3,2,1,0:T(8,128)(2,1)}, u32[]{:S(2)}, u32[]{:S(2)}) collective-permute-start(bf16[3,16,8,512]{3,2,1,0:T(8,128)(2,1)} %broadcast_select_fusion.2), channel_id=1, source_target_pairs={{4,0},{5,1},{6,2},{7,3},{8,4},{9,5},{10,6},{11,7},{12,8},{13,9},{1... | collective-permute-start | bytes 1179656 | tf_op jit(solution)/shard_map/ppermute | solution.py:17
  58.8 840.0 %reduce-scatter.2.cloned.1.call-start = ((), (), s32[]{:S(2)}) async-start(), calls=%async_computation.2 | async-start | bytes 2162688 | tf_op jit(solution)/shard_map/reduce_scatter | solution.py:214
  59.8 109.5 %collective-permute-start.17 = (bf16[11,7,8,512]{3,2,1,0:T(8,128)(2,1)}, bf16[11,7,8,512]{3,2,1,0:T(8,128)(2,1)}, u32[]{:S(2)}, u32[]{:S(2)}) collective-permute-start(bf16[11,7,8,512]{3,2,1,0:T(8,128)(2,1)} %slice.113), channel_id=1, source_target_pairs={{1,0},{2,1},{3,2},{4,3},{5,4},{6,5},{7,6},{8,7},{9,8},{10,9},{11,1... | collective-permute-start | bytes 1892360 | tf_op jit(solution)/shard_map/ppermute | solution.py:17
  60.8 104.0 %collective-permute-start.4 = (bf16[3,16,8,512]{3,2,1,0:T(8,128)(2,1)S(1)}, bf16[3,16,8,512]{3,2,1,0:T(8,128)(2,1)}, u32[]{:S(2)}, u32[]{:S(2)}) collective-permute-start(bf16[3,16,8,512]{3,2,1,0:T(8,128)(2,1)S(1)} %broadcast_select_fusion.3), channel_id=1, source_target_pairs={{4,0},{5,1},{6,2},{7,3},{8,4},{9,5},{10,6},{11,7},{12,8},{13,9},{1... | collective-permute-start | bytes 1179656 | tf_op jit(solution)/shard_map/ppermute | solution.py:17
  80.1 86.5 %collective-permute-start.21 = (bf16[3,16,8,512]{3,2,1,0:T(8,128)(2,1)}, bf16[3,16,8,512]{3,2,1,0:T(8,128)(2,1)}, u32[]{:S(2)}, u32[]{:S(2)}) collective-permute-start(bf16[3,16,8,512]{3,2,1,0:T(8,128)(2,1)} %broadcast_select_fusion.4), channel_id=1, source_target_pairs={{8,0},{9,1},{10,2},{11,3},{12,4},{13,5},{14,6},{15,7},{16,8},{17,9... | collective-permute-start | bytes 1179656 | tf_op jit(solution)/shard_map/ppermute | solution.py:17
  164.8 26.8 %collective-permute-start.1 = (bf16[11,7,8,512]{3,2,1,0:T(8,128)(2,1)S(1)}, bf16[11,7,8,512]{3,2,1,0:T(8,128)(2,1)S(1)}, u32[]{:S(2)}, u32[]{:S(2)}) collective-permute-start(bf16[11,7,8,512]{3,2,1,0:T(8,128)(2,1)S(1)} %slice.104), channel_id=1, source_target_pairs={{1,0},{2,1},{3,2},{4,3},{5,4},{6,5},{7,6},{8,7},{9,8},{10,9},{11,1... | collective-permute-start | bytes 1892360 | tf_op jit(solution)/shard_map/ppermute | solution.py:17
  165.9 24.8 %collective-permute-start.5 = (bf16[3,16,8,512]{3,2,1,0:T(8,128)(2,1)S(1)}, bf16[3,16,8,512]{3,2,1,0:T(8,128)(2,1)S(1)}, u32[]{:S(2)}, u32[]{:S(2)}) collective-permute-start(bf16[3,16,8,512]{3,2,1,0:T(8,128)(2,1)S(1)} %broadcast_select_fusion.5), channel_id=1, source_target_pairs={{8,0},{9,1},{10,2},{11,3},{12,4},{13,5},{14,6},{15,7},{16,8},{17,9... | collective-permute-start | bytes 1179656 | tf_op jit(solution)/shard_map/ppermute | solution.py:17
  167.6 23.8 %collective-permute-start.22 = (bf16[3,16,8,512]{3,2,1,0:T(8,128)(2,1)S(1)}, bf16[3,16,8,512]{3,2,1,0:T(8,128)(2,1)S(1)}, u32[]{:S(2)}, u32[]{:S(2)}) collective-permute-start(bf16[3,16,8,512]{3,2,1,0:T(8,128)(2,1)S(1)} %broadcast_select_fusion.6), channel_id=1, source_target_pairs={{16,0},{17,1},{18,2},{19,3},{20,4},{21,5},{22,6},{23,7},{24,8},{25... | collective-permute-start | bytes 1179656 | tf_op jit(solution)/shard_map/ppermute | solution.py:17
  190.7 9.1 collective-permute-start.6
  191.5 8.4 collective-permute-start.23
  199.8 15.3 %collective-permute-start.7 = (bf16[3,16,8,512]{3,2,1,0:T(8,128)(2,1)S(1)}, bf16[3,16,8,512]{3,2,1,0:T(8,128)(2,1)S(1)}, u32[]{:S(2)}, u32[]{:S(2)}) collective-permute-start(bf16[3,16,8,512]{3,2,1,0:T(8,128)(2,1)S(1)} %broadcast_select_fusion.9), channel_id=1, source_target_pairs={{1,0},{2,1},{3,2},{4,3},{5,4},{6,5},{7,6},{8,7},{9,8},{10,9},{11,1... | collective-permute-start | bytes 1179656 | tf_op jit(solution)/shard_map/ppermute | solution.py:17
  200.2 2.1 copy-start.10
  201.2 1.0 copy-start.1
  215.6 1.6 copy-start.13
  308.6 3.3 copy-start
  344.8 3.2 copy-start.8
  373.5 17.1 %copy-start.7 = (bf16[4,16,256,32]{2,3,1,0:T(8,128)(2,1)S(1)}, bf16[4,16,256,32]{2,3,1,0:T(8,128)(2,1)}, u32[]{:S(2)}) copy-start(bf16[4,16,256,32]{2,3,1,0:T(8,128)(2,1)} %fusion.31) | copy-start | bytes 3145732
  404.5 7.1 copy-start.15
  411.5 4.2 copy-start.2
  415.7 1.3 copy-start.6
  415.8 1.3 copy-start.11
  416.9 2.0 copy-start.3
  416.9 2.4 copy-start.9
  416.9 16.7 %collective-permute-start.24 = (bf16[3,16,8,512]{3,2,1,0:T(8,128)(2,1)S(1)}, bf16[3,16,8,512]{3,2,1,0:T(8,128)(2,1)S(1)}, u32[]{:S(2)}, u32[]{:S(2)}) collective-permute-start(bf16[3,16,8,512]{3,2,1,0:T(8,128)(2,1)S(1)} %bitcast.124), channel_id=1, source_target_pairs={{224,0},{0,32},{32,64},{64,96},{96,128},{128,160},{160,192},{192,2... | collective-permute-start | bytes 1179656 | tf_op jit(solution)/shard_map/ppermute | solution.py:17
  418.6 23.1 %collective-permute-start.8 = (bf16[3,16,8,512]{3,2,1,0:T(8,128)(2,1)}, bf16[3,16,8,512]{3,2,1,0:T(8,128)(2,1)S(1)}, u32[]{:S(2)}, u32[]{:S(2)}) collective-permute-start(bf16[3,16,8,512]{3,2,1,0:T(8,128)(2,1)} %bitcast.13), channel_id=1, source_target_pairs={{224,0},{0,32},{32,64},{64,96},{96,128},{128,160},{160,192},{192,2... | collective-permute-start | bytes 1179656 | tf_op jit(solution)/shard_map/ppermute | solution.py:17
  433.6 8.2 collective-permute-start.25
  436.0 574.4 %all-reduce.2.cloned.1.call-start = ((), (), s32[]{:S(2)}) async-start(), calls=%async_computation.3 | async-start | bytes 131072 | tf_op jit(solution)/shard_map/psum | solution.py:213
  441.7 358.5 %collective-permute-start.9 = (bf16[3,16,8,512]{3,2,1,0:T(8,128)(2,1)S(1)}, bf16[3,16,8,512]{3,2,1,0:T(8,128)(2,1)}, u32[]{:S(2)}, u32[]{:S(2)}) collective-permute-start(bf16[3,16,8,512]{3,2,1,0:T(8,128)(2,1)S(1)} %collective-permute-done.8), channel_id=1, source_target_pairs={{1,0},{2,1},{3,2},{4,3},{5,4},{6,5},{7,6},{8,7},{9,8},{10,9},{11,1... | collective-permute-start | bytes 1179656 | tf_op jit(solution)/shard_map/ppermute | solution.py:17
  442.5 365.9 %collective-permute-start.26 = (bf16[3,16,8,512]{3,2,1,0:T(8,128)(2,1)}, bf16[3,16,8,512]{3,2,1,0:T(8,128)(2,1)}, u32[]{:S(2)}, u32[]{:S(2)}) collective-permute-start(bf16[3,16,8,512]{3,2,1,0:T(8,128)(2,1)} %broadcast_select_fusion.10), channel_id=1, source_target_pairs={{2,0},{3,1},{4,2},{5,3},{6,4},{7,5},{8,6},{9,7},{10,8},{11,9},{12,... | collective-permute-start | bytes 1179656 | tf_op jit(solution)/shard_map/ppermute | solution.py:17
  800.3 25.6 %collective-permute-start.10 = (bf16[3,16,8,512]{3,2,1,0:T(8,128)(2,1)S(1)}, bf16[3,16,8,512]{3,2,1,0:T(8,128)(2,1)S(1)}, u32[]{:S(2)}, u32[]{:S(2)}) collective-permute-start(bf16[3,16,8,512]{3,2,1,0:T(8,128)(2,1)S(1)} %broadcast_select_fusion.11), channel_id=1, source_target_pairs={{2,0},{3,1},{4,2},{5,3},{6,4},{7,5},{8,6},{9,7},{10,8},{11,9},{12,... | collective-permute-start | bytes 1179656 | tf_op jit(solution)/shard_map/ppermute | solution.py:17
  809.5 30.7 %collective-permute-start.27 = (bf16[3,16,8,512]{3,2,1,0:T(8,128)(2,1)S(1)}, bf16[3,16,8,512]{3,2,1,0:T(8,128)(2,1)S(1)}, u32[]{:S(2)}, u32[]{:S(2)}) collective-permute-start(bf16[3,16,8,512]{3,2,1,0:T(8,128)(2,1)S(1)} %broadcast_select_fusion.12), channel_id=1, source_target_pairs={{4,0},{5,1},{6,2},{7,3},{8,4},{9,5},{10,6},{11,7},{12,8},{13,9},{1... | collective-permute-start | bytes 1179656 | tf_op jit(solution)/shard_map/ppermute | solution.py:17
  826.0 34.2 %collective-permute-start.11 = (bf16[3,16,8,512]{3,2,1,0:T(8,128)(2,1)S(1)}, bf16[3,16,8,512]{3,2,1,0:T(8,128)(2,1)S(1)}, u32[]{:S(2)}, u32[]{:S(2)}) collective-permute-start(bf16[3,16,8,512]{3,2,1,0:T(8,128)(2,1)S(1)} %broadcast_select_fusion.13), channel_id=1, source_target_pairs={{4,0},{5,1},{6,2},{7,3},{8,4},{9,5},{10,6},{11,7},{12,8},{13,9},{1... | collective-permute-start | bytes 1179656 | tf_op jit(solution)/shard_map/ppermute | solution.py:17
  840.3 29.5 %collective-permute-start.28 = (bf16[3,16,8,512]{3,2,1,0:T(8,128)(2,1)S(1)}, bf16[3,16,8,512]{3,2,1,0:T(8,128)(2,1)S(1)}, u32[]{:S(2)}, u32[]{:S(2)}) collective-permute-start(bf16[3,16,8,512]{3,2,1,0:T(8,128)(2,1)S(1)} %broadcast_select_fusion.14), channel_id=1, source_target_pairs={{8,0},{9,1},{10,2},{11,3},{12,4},{13,5},{14,6},{15,7},{16,8},{17,9... | collective-permute-start | bytes 1179656 | tf_op jit(solution)/shard_map/ppermute | solution.py:17
  840.4 29.5 %collective-permute-start.31 = (bf16[11,7,8,512]{3,2,1,0:T(8,128)(2,1)S(1)}, bf16[11,7,8,512]{3,2,1,0:T(8,128)(2,1)S(1)}, u32[]{:S(2)}, u32[]{:S(2)}) collective-permute-start(bf16[11,7,8,512]{3,2,1,0:T(8,128)(2,1)S(1)} %pad_maximum_fusion.1), channel_id=1, source_target_pairs={{31,0},{0,1},{1,2},{2,3},{3,4},{4,5},{5,6},{6,7},{7,8},{8,9},{9,10... | collective-permute-start | bytes 1892360 | tf_op jit(solution)/shard_map/ppermute | solution.py:17
  840.6 44.8 %collective-permute-start.15 = (bf16[11,7,8,512]{3,2,1,0:T(8,128)(2,1)S(1)}, bf16[11,7,8,512]{3,2,1,0:T(8,128)(2,1)S(1)}, u32[]{:S(2)}, u32[]{:S(2)}) collective-permute-start(bf16[11,7,8,512]{3,2,1,0:T(8,128)(2,1)S(1)} %pad_maximum_fusion.2), channel_id=1, source_target_pairs={{31,0},{0,1},{1,2},{2,3},{3,4},{4,5},{5,6},{6,7},{7,8},{8,9},{9,10... | collective-permute-start | bytes 1892360 | tf_op jit(solution)/shard_map/ppermute | solution.py:17
  860.2 17.9 %collective-permute-start.12 = (bf16[3,16,8,512]{3,2,1,0:T(8,128)(2,1)S(1)}, bf16[3,16,8,512]{3,2,1,0:T(8,128)(2,1)S(1)}, u32[]{:S(2)}, u32[]{:S(2)}) collective-permute-start(bf16[3,16,8,512]{3,2,1,0:T(8,128)(2,1)S(1)} %broadcast_select_fusion.15), channel_id=1, source_target_pairs={{8,0},{9,1},{10,2},{11,3},{12,4},{13,5},{14,6},{15,7},{16,8},{17,9... | collective-permute-start | bytes 1179656 | tf_op jit(solution)/shard_map/ppermute | solution.py:17
  869.8 10.9 %collective-permute-start.29 = (bf16[3,16,8,512]{3,2,1,0:T(8,128)(2,1)S(1)}, bf16[3,16,8,512]{3,2,1,0:T(8,128)(2,1)S(1)}, u32[]{:S(2)}, u32[]{:S(2)}) collective-permute-start(bf16[3,16,8,512]{3,2,1,0:T(8,128)(2,1)S(1)} %broadcast_select_fusion.16), channel_id=1, source_target_pairs={{16,0},{17,1},{18,2},{19,3},{20,4},{21,5},{22,6},{23,7},{24,8},{25... | collective-permute-start | bytes 1179656 | tf_op jit(solution)/shard_map/ppermute | solution.py:17
  878.1 11.0 %collective-permute-start.13 = (bf16[3,16,8,512]{3,2,1,0:T(8,128)(2,1)S(1)}, bf16[3,16,8,512]{3,2,1,0:T(8,128)(2,1)S(1)}, u32[]{:S(2)}, u32[]{:S(2)}) collective-permute-start(bf16[3,16,8,512]{3,2,1,0:T(8,128)(2,1)S(1)} %broadcast_select_fusion.17), channel_id=1, source_target_pairs={{16,0},{17,1},{18,2},{19,3},{20,4},{21,5},{22,6},{23,7},{24,8},{25... | collective-permute-start | bytes 1179656 | tf_op jit(solution)/shard_map/ppermute | solution.py:17
  880.8 12.4 %collective-permute-start.30 = (bf16[3,16,8,512]{3,2,1,0:T(8,128)(2,1)S(1)}, bf16[3,16,8,512]{3,2,1,0:T(8,128)(2,1)S(1)}, u32[]{:S(2)}, u32[]{:S(2)}) collective-permute-start(bf16[3,16,8,512]{3,2,1,0:T(8,128)(2,1)S(1)} %broadcast_select_fusion.18), channel_id=1, source_target_pairs={{1,0},{2,1},{3,2},{4,3},{5,4},{6,5},{7,6},{8,7},{9,8},{10,9},{11,1... | collective-permute-start | bytes 1179656 | tf_op jit(solution)/shard_map/ppermute | solution.py:17
  889.2 9.2 collective-permute-start.14
Sparse Core Ops, SparseCore 0:
  58.9 71.1 all-gather.3
  436.1 117.9 reduce-scatter.1
  899.0 111.2 all-reduce.1
